TPU v7x, 32 devices: a whole 2x2x4 slice. The times are simulated.
32 devices in a mesh: lat: 4 (over z), lon: 8 (over y, x, core).
Axes of the slice: x: 2, y: 2, z: 4, core: 2. Of those that a mesh axis runs over, the one named last changes fastest.
Arguments:
- covariance: float32 [4, 4, 128, 128], P('lat', None, 'lon'), may hold values from -6 to 6
- winds: float32 [2, 3, 4, 128], P(None, None, None, 'lon'), may hold values from -0.35 to 0.35
- diffusivity: float32 [4, 128], P(None, 'lon'), may hold values from 0.01 to 0.07
- cutoff: int32 [4], replicated, may hold values from 0 to 1, as said below
Outputs:
- forecast: float32 [4, 4, 128, 128], P('lat', None, 'lon')
Inputs may be any that keep to these rules, and one draw needn't show every extreme that they name: Some latitude has cutoff 1 and some other has 0.
All inputs are finite; a program needn't handle non-finite values.
Results may differ from a plain program's by a relative error of at most 0.00002.
Values sent between devices are 32-bit elements; how exact they have to be, the bound alone decides.
No kernel may reach another device: no remote copies, remote signals or barrier semaphores. Data moves between devices by JAX's collectives and lax.ppermute only.
A program may use at most 192 MiB of HBM per device.

v0:
```python
import jax
import jax.numpy as jnp
from jax import lax
from jax.sharding import PartitionSpec as P

STEPS = 3


def extended_2(block, sides, width):
    for axis, dim in sides:
        count = lax.axis_size(axis)
        forward = [(i, i + 1) for i in range(count - 1)]
        forward.append((count - 1, 0))
        backward = [(target, source) for source, target in forward]
        low = lax.ppermute(
            lax.slice_in_dim(block, block.shape[dim] - width, None, axis=dim), axis, forward
        )
        high = lax.ppermute(lax.slice_in_dim(block, 0, width, axis=dim), axis, backward)
        block = jnp.concatenate([low, block, high], axis=dim)
    return block


def from_behind(shard, axis, by):
    length = lax.axis_size(axis)
    pairs = [(i, i + by) for i in range(length) if 0 <= i + by < length]
    return lax.ppermute(shard, axis, pairs)


def advance(extended, east_wind, north_wind, spread):
    center = extended[:, :, 1:-1]
    western = extended[:, :, :-2]
    eastern = extended[:, :, 2:]
    zeros_row = jnp.zeros_like(center[:, :1])
    southern = jnp.concatenate([zeros_row, center[:, :-1]], axis=1)
    northern = jnp.concatenate([center[:, 1:], zeros_row], axis=1)
    east_wind = east_wind[None, :, :, None]
    north_wind = north_wind[None, :, :, None]
    spread = spread[None, :, :, None]
    transport = (
        jnp.maximum(east_wind, 0.0) * (center - western)
        + jnp.minimum(east_wind, 0.0) * (eastern - center)
        + jnp.maximum(north_wind, 0.0) * (center - southern)
        + jnp.minimum(north_wind, 0.0) * (northern - center)
    )
    return center - transport + spread * (eastern + western + northern + southern - 4.0 * center)


def propagate(state_field, widened):
    lon_local = state_field.shape[2]
    extended = extended_2(state_field, (("lon", 2),), STEPS)
    for substep in range(STEPS):
        out_width = lon_local + 2 * (STEPS - substep - 1)
        offset_at = substep + 1
        extended = advance(
            extended,
            widened[substep, :, offset_at : offset_at + out_width],
            widened[STEPS + substep, :, offset_at : offset_at + out_width],
            widened[2 * STEPS, :, offset_at : offset_at + out_width],
        )
    return extended


def relayout(block, reach_rows):
    row_count = block.shape[0]
    lat_count = block.shape[1]
    swapped = lax.all_to_all(block, "lon", split_axis=3, concat_axis=2, tiled=True)
    lon_count = swapped.shape[2]
    col_count = swapped.shape[3]
    block_count = lat_count // row_count
    device_index = lax.axis_index("lat")
    reach_blocks = min((reach_rows + row_count - 1) // row_count, block_count - 1)
    tile_blocks = swapped.reshape(row_count, block_count, row_count, lon_count, col_count)

    def piece_for(offset):
        target = jnp.clip(device_index + offset, 0, block_count - 1)
        return lax.dynamic_index_in_dim(tile_blocks, target, axis=1, keepdims=False)

    own_piece = piece_for(0)
    received = []
    for offset in range(-reach_blocks, reach_blocks + 1):
        if offset == 0:
            received.append(own_piece)
        else:
            received.append(from_behind(piece_for(offset), "lat", offset))
    window = jnp.stack(received[::-1], axis=0)
    padded = jnp.zeros(
        (block_count + 2 * reach_blocks, row_count, row_count, lon_count, col_count), jnp.float32
    )
    padded = lax.dynamic_update_slice_in_dim(padded, window, device_index, 0)
    regrouped = padded[reach_blocks : reach_blocks + block_count].reshape(
        lat_count, row_count, lon_count, col_count
    )
    return jnp.transpose(regrouped, (1, 0, 3, 2))


def per_device(covariance, winds, diffusivity, cutoff):
    row_count = covariance.shape[0]
    lat_count = covariance.shape[1]
    lon_local = covariance.shape[2]
    band_rows = lat_count // 4
    device_index = lax.axis_index("lat")
    lat_local = device_index * row_count + jnp.arange(row_count, dtype=jnp.int32)
    lat_all = jnp.arange(lat_count, dtype=jnp.int32)
    cut_local = lax.dynamic_slice_in_dim(cutoff, device_index * row_count, row_count)
    keep_first = jnp.abs(lat_all[None, :] - lat_local[:, None]) <= cutoff[None, :]
    keep_second = jnp.abs(lat_all[None, :] - lat_local[:, None]) <= cut_local[:, None]
    stacked = jnp.concatenate(
        [winds.reshape(2 * STEPS, lat_count, lon_local), diffusivity[None]], axis=0
    )
    widened = extended_2(stacked, (("lon", 2),), STEPS)
    state_field = jnp.where(keep_first[:, :, None, None], covariance, 0.0)
    state_field = propagate(state_field, widened)
    state_field = relayout(state_field, band_rows + STEPS)
    state_field = propagate(state_field, widened)
    state_field = jnp.where(keep_second[:, :, None, None], state_field, 0.0)
    return relayout(state_field, band_rows)


def solution(mesh):
    in_specs = (P("lat", None, "lon", None), P(None, None, None, "lon"), P(None, "lon"), P())
    out_specs = P("lat", None, "lon", None)
    return jax.shard_map(
        per_device, mesh=mesh, in_specs=in_specs, out_specs=out_specs, check_vma=False
    )
```

profile of v0, /device:TPU:0, one launch (start us, length us, event | category | flops | bytes accessed | tf_op | source)
XLA Modules:
  0.0 67.6 jit_solution(5714886319299607555)
XLA Ops:
  0.0 0.0 copy-start.2
  0.0 0.7 copy-done.2
  0.7 0.6 dynamic_slice.34
  1.2 0.7 fusion.50
  1.9 0.8 %broadcast_select_fusion = f32[1,4,16,128]{3,2,1,0:T(8,128)S(1)} fusion(f32[1,4,16,128]{3,2,1,0:T(8,128)} %param.4, pred[4]{0:T(512)(128)(4,1)S(1)} %get-tuple-element.51), kind=kLoop, calls=%fused_computation.86 | loop fusion | flops 8192 | bytes 65540 | tf_op jit(solution)/shard_map/jit(_where)/select_n | solution.py:111
  2.7 0.0 copy-start
  2.7 0.5 collective-permute-start
  3.3 0.0 copy-start.1
  3.3 2.9 %collective-permute-start.1 = (f32[1,4,3,128]{3,2,1,0:T(4,128)S(1)}, f32[1,4,3,128]{3,2,1,0:T(4,128)S(1)}, u32[]{:S(2)}, u32[]{:S(2)}) collective-permute-start(f32[1,4,3,128]{3,2,1,0:T(4,128)S(1)} %get-tuple-element.44), channel_id=1, source_target_pairs={{1,0},{2,1},{3,2},{4,3},{5,4},{6,5},{7,6},{0,7},{9,8},{10,9},{11,1... | collective-permute-start | bytes 18440 | tf_op jit(solution)/shard_map/ppermute | solution.py:18
  6.2 0.0 copy-done
  6.2 0.0 copy-done.1
  6.2 0.1 slice_maximum_fusion
  6.3 0.3 collective-permute-start.2
  6.6 2.3 %collective-permute-start.3 = (f32[7,4,3]{2,1,0:T(4,128)S(1)}, f32[7,4,3]{2,1,0:T(4,128)S(1)}, u32[]{:S(2)}, u32[]{:S(2)}) collective-permute-start(f32[7,4,3]{2,1,0:T(4,128)S(1)} %get-tuple-element.46), channel_id=1, source_target_pairs={{1,0},{2,1},{3,2},{4,3},{5,4},{6,5},{7,6},{0,7},{9,8},{10,9},{11,1... | collective-permute-start | bytes 1016 | tf_op jit(solution)/shard_map/ppermute | solution.py:18
  9.0 1.4 %collective-permute-done.2 = f32[7,4,3]{2,1,0:T(4,128)S(1)} collective-permute-done((f32[7,4,3]{2,1,0:T(4,128)S(1)}, f32[7,4,3]{2,1,0:T(4,128)S(1)}, u32[]{:S(2)}, u32[]{:S(2)}) %collective-permute-start.2) | collective-permute-done | bytes 368 | tf_op jit(solution)/shard_map/ppermute | solution.py:15
  10.4 0.0 collective-permute-done.3
  10.4 0.1 maximum_bitcast_fusion.6
  10.5 0.1 maximum_bitcast_fusion.4
  10.6 0.0 collective-permute-done
  10.6 0.0 collective-permute-done.1
  10.6 0.1 fusion.4
  10.8 0.1 fusion.12
  10.9 0.1 fusion.36
  11.0 0.1 copy.36
  11.2 0.8 %reshape.186 = f32[8,1,1024]{2,1,0:T(1,128)} reshape(f32[128,1,4,16]{3,2,1,0:T(4,128)S(1)} %bitcast.89) | data formatting | bytes 65536
  12.0 4.6 %all-to-all-start = ((f32[8,1,1024]{2,1,0:T(1,128)}), f32[8,1,1024]{2,1,0:T(1,128)S(1)}, u32[]{:S(2)}, u32[]{:S(2)}) async-start(f32[8,1,1024]{2,1,0:T(1,128)} %reshape.186), calls=%async_computation | async-start | bytes 65536 | tf_op jit(solution)/shard_map/all_to_all | solution.py:66
  16.7 4.8 %all-to-all-done = f32[8,1,1024]{2,1,0:T(1,128)S(1)} async-done(((f32[8,1,1024]{2,1,0:T(1,128)}), f32[8,1,1024]{2,1,0:T(1,128)S(1)}, u32[]{:S(2)}, u32[]{:S(2)}) %all-to-all-start) | async-done | bytes 32800 | tf_op jit(solution)/shard_map/all_to_all | solution.py:66
  21.5 0.5 broadcast.178
  22.0 0.7 %reduce = f32[8,1024]{1,0:T(8,128)S(1)} reduce(f32[8,1,1024]{2,1,0:T(1,128)S(1)} %all-to-all-done, f32[]{:T(128)} %broadcast.178), dimensions={1}, to_apply=%all_to_all.22.reduce_sub_computation | reduce | bytes 65540 | tf_op jit(solution)/shard_map/all_to_all | solution.py:66
  22.7 0.2 reshape.187
  23.0 0.2 copy.37
  23.1 0.1 reshape.182
  23.3 5.5 %collective-permute-start.4 = (f32[1,1,128,16]{2,3,1,0:T(8,128)S(1)}, f32[1,1,128,16]{2,3,1,0:T(8,128)S(1)}, u32[]{:S(2)}, u32[]{:S(2)}) collective-permute-start(f32[1,1,128,16]{2,3,1,0:T(8,128)S(1)} %get-tuple-element.42), channel_id=1, source_target_pairs={{0,24},{1,25},{2,26},{3,27},{4,28},{5,29},{6,30},{7,31}} | collective-permute-start | bytes 24584 | tf_op jit(solution)/shard_map/ppermute | solution.py:26
  28.8 1.3 %collective-permute-start.5 = (f32[1,1,128,16]{2,3,1,0:T(8,128)S(1)}, f32[1,1,128,16]{2,3,1,0:T(8,128)S(1)}, u32[]{:S(2)}, u32[]{:S(2)}) collective-permute-start(f32[1,1,128,16]{2,3,1,0:T(8,128)S(1)} %get-tuple-element.41), channel_id=1, source_target_pairs={{0,16},{8,24},{1,17},{9,25},{2,18},{10,26},{3,19},{11,27},{4,20},{... | collective-permute-start | bytes 24584 | tf_op jit(solution)/shard_map/ppermute | solution.py:26
  30.1 2.5 %collective-permute-start.6 = (f32[1,1,128,16]{2,3,1,0:T(8,128)S(1)}, f32[1,1,128,16]{2,3,1,0:T(8,128)S(1)}, u32[]{:S(2)}, u32[]{:S(2)}) collective-permute-start(f32[1,1,128,16]{2,3,1,0:T(8,128)S(1)} %get-tuple-element.40), channel_id=1, source_target_pairs={{0,8},{8,16},{16,24},{1,9},{9,17},{17,25},{2,10},{10,18},{18,26},{... | collective-permute-start | bytes 24584 | tf_op jit(solution)/shard_map/ppermute | solution.py:26
  32.6 0.0 collective-permute-done.4
  32.6 0.0 collective-permute-done.5
  32.6 1.3 %collective-permute-done.6 = f32[1,1,128,16]{2,3,1,0:T(8,128)S(1)} collective-permute-done((f32[1,1,128,16]{2,3,1,0:T(8,128)S(1)}, f32[1,1,128,16]{2,3,1,0:T(8,128)S(1)}, u32[]{:S(2)}, u32[]{:S(2)}) %collective-permute-start.6) | collective-permute-done | bytes 8224 | tf_op jit(solution)/shard_map/ppermute | solution.py:26
  33.9 1.3 %collective-permute-start.7 = (f32[1,1,128,16]{2,3,1,0:T(8,128)S(1)}, f32[1,1,128,16]{2,3,1,0:T(8,128)S(1)}, u32[]{:S(2)}, u32[]{:S(2)}) collective-permute-start(f32[1,1,128,16]{2,3,1,0:T(8,128)S(1)} %get-tuple-element.38), channel_id=1, source_target_pairs={{8,0},{16,8},{24,16},{9,1},{17,9},{25,17},{10,2},{18,10},{26,18},{... | collective-permute-start | bytes 24584 | tf_op jit(solution)/shard_map/ppermute | solution.py:26
  35.2 1.3 %collective-permute-start.8 = (f32[1,1,128,16]{2,3,1,0:T(8,128)S(1)}, f32[1,1,128,16]{2,3,1,0:T(8,128)S(1)}, u32[]{:S(2)}, u32[]{:S(2)}) collective-permute-start(f32[1,1,128,16]{2,3,1,0:T(8,128)S(1)} %get-tuple-element.37), channel_id=1, source_target_pairs={{16,0},{24,8},{17,1},{25,9},{18,2},{26,10},{19,3},{27,11},{20,4},{... | collective-permute-start | bytes 24584 | tf_op jit(solution)/shard_map/ppermute | solution.py:26
  36.5 1.3 %collective-permute-start.9 = (f32[1,1,128,16]{2,3,1,0:T(8,128)S(1)}, f32[1,1,128,16]{2,3,1,0:T(8,128)S(1)}, u32[]{:S(2)}, u32[]{:S(2)}) collective-permute-start(f32[1,1,128,16]{2,3,1,0:T(8,128)S(1)} %get-tuple-element.36), channel_id=1, source_target_pairs={{24,0},{25,1},{26,2},{27,3},{28,4},{29,5},{30,6},{31,7}} | collective-permute-start | bytes 24584 | tf_op jit(solution)/shard_map/ppermute | solution.py:26
  37.8 1.9 %collective-permute-done.7 = f32[1,1,128,16]{2,3,1,0:T(8,128)S(1)} collective-permute-done((f32[1,1,128,16]{2,3,1,0:T(8,128)S(1)}, f32[1,1,128,16]{2,3,1,0:T(8,128)S(1)}, u32[]{:S(2)}, u32[]{:S(2)}) %collective-permute-start.7) | collective-permute-done | bytes 8224 | tf_op jit(solution)/shard_map/ppermute | solution.py:26
  39.7 2.7 %collective-permute-done.8 = f32[1,1,128,16]{2,3,1,0:T(8,128)S(1)} collective-permute-done((f32[1,1,128,16]{2,3,1,0:T(8,128)S(1)}, f32[1,1,128,16]{2,3,1,0:T(8,128)S(1)}, u32[]{:S(2)}, u32[]{:S(2)}) %collective-permute-start.8) | collective-permute-done | bytes 8224 | tf_op jit(solution)/shard_map/ppermute | solution.py:26
  42.5 2.8 %collective-permute-done.9 = f32[1,1,128,16]{2,3,1,0:T(8,128)S(1)} collective-permute-done((f32[1,1,128,16]{2,3,1,0:T(8,128)S(1)}, f32[1,1,128,16]{2,3,1,0:T(8,128)S(1)}, u32[]{:S(2)}, u32[]{:S(2)}) %collective-permute-start.9) | collective-permute-done | bytes 8224 | tf_op jit(solution)/shard_map/ppermute | solution.py:26
  45.4 0.1 collective-permute-start.10
  45.4 2.6 %collective-permute-start.11 = (f32[1,4,3,128]{3,2,1,0:T(4,128)S(1)}, f32[1,4,3,128]{3,2,1,0:T(4,128)S(1)}, u32[]{:S(2)}, u32[]{:S(2)}) collective-permute-start(f32[1,4,3,128]{3,2,1,0:T(4,128)S(1)} %get-tuple-element.35), channel_id=1, source_target_pairs={{1,0},{2,1},{3,2},{4,3},{5,4},{6,5},{7,6},{0,7},{9,8},{10,9},{11,1... | collective-permute-start | bytes 18440 | tf_op jit(solution)/shard_map/ppermute | solution.py:18
  48.1 1.4 %collective-permute-done.10 = f32[1,4,3,128]{3,2,1,0:T(4,128)S(1)} collective-permute-done((f32[1,4,3,128]{3,2,1,0:T(4,128)S(1)}, f32[1,4,3,128]{3,2,1,0:T(4,128)S(1)}, u32[]{:S(2)}, u32[]{:S(2)}) %collective-permute-start.10) | collective-permute-done | bytes 6176 | tf_op jit(solution)/shard_map/ppermute | solution.py:15
  49.5 0.0 collective-permute-done.11
  49.5 0.1 fusion.20
  49.6 0.1 fusion.28
  49.8 0.1 fusion.45
  49.9 0.1 copy.39
  50.1 0.2 reshape.188
  50.3 8.5 %all_to_all.30 = f32[8,1,1024]{2,1,0:T(1,128)S(1)} all-to-all(f32[8,1,1024]{2,1,0:T(1,128)S(1)} %reshape.188), channel_id=1, replica_groups=mesh['lat'=4,'lon'=8] {'lon'}, dimensions={0} | all-to-all | bytes 65536 | tf_op jit(solution)/shard_map/all_to_all | solution.py:66
  58.8 0.7 %reduce.1 = f32[8,1024]{1,0:T(8,128)S(1)} reduce(f32[8,1,1024]{2,1,0:T(1,128)S(1)} %all_to_all.30, f32[]{:T(128)} %broadcast.178), dimensions={1}, to_apply=%all_to_all.25.reduce_sub_computation | reduce | bytes 65540 | tf_op jit(solution)/shard_map/all_to_all | solution.py:66
  59.5 0.2 reshape.189
  59.8 0.2 copy.40
  59.9 0.1 reshape.184
  60.1 1.3 %collective-permute-start.12 = (f32[1,1,128,16]{2,3,1,0:T(8,128)S(1)}, f32[1,1,128,16]{2,3,1,0:T(8,128)S(1)}, u32[]{:S(2)}, u32[]{:S(2)}) collective-permute-start(f32[1,1,128,16]{2,3,1,0:T(8,128)S(1)} %get-tuple-element.31), channel_id=1, source_target_pairs={{0,8},{8,16},{16,24},{1,9},{9,17},{17,25},{2,10},{10,18},{18,26},{... | collective-permute-start | bytes 24584 | tf_op jit(solution)/shard_map/ppermute | solution.py:26
  61.4 1.3 %collective-permute-start.13 = (f32[1,1,128,16]{2,3,1,0:T(8,128)S(1)}, f32[1,1,128,16]{2,3,1,0:T(8,128)S(1)}, u32[]{:S(2)}, u32[]{:S(2)}) collective-permute-start(f32[1,1,128,16]{2,3,1,0:T(8,128)S(1)} %get-tuple-element.32), channel_id=1, source_target_pairs={{8,0},{16,8},{24,16},{9,1},{17,9},{25,17},{10,2},{18,10},{26,18},{... | collective-permute-start | bytes 24584 | tf_op jit(solution)/shard_map/ppermute | solution.py:26
  62.7 0.0 collective-permute-done.12
  62.7 4.2 %collective-permute-done.13 = f32[1,1,128,16]{2,3,1,0:T(8,128)S(1)} collective-permute-done((f32[1,1,128,16]{2,3,1,0:T(8,128)S(1)}, f32[1,1,128,16]{2,3,1,0:T(8,128)S(1)}, u32[]{:S(2)}, u32[]{:S(2)}) %collective-permute-start.13) | collective-permute-done | bytes 8224 | tf_op jit(solution)/shard_map/ppermute | solution.py:26
  66.9 0.6 slice_bitcast_fusion
  (27 shorter events, 0.2 us)
Async XLA Ops:
  0.0 0.7 copy-start.2
  2.7 3.5 %copy-start = (f32[2,3,4,16]{3,2,1,0:T(4,128)S(1)}, f32[2,3,4,16]{3,2,1,0:T(4,128)}, u32[]{:S(2)}) copy-start(f32[2,3,4,16]{3,2,1,0:T(4,128)} %param.5) | copy-start | bytes 4612
  2.7 7.8 %collective-permute-start = (f32[1,4,3,128]{3,2,1,0:T(4,128)S(1)}, f32[1,4,3,128]{3,2,1,0:T(4,128)S(1)}, u32[]{:S(2)}, u32[]{:S(2)}) collective-permute-start(f32[1,4,3,128]{3,2,1,0:T(4,128)S(1)} %get-tuple-element.43), channel_id=1, source_target_pairs={{0,1},{1,2},{2,3},{3,4},{4,5},{5,6},{6,7},{7,0},{8,9},{9,10},{10,1... | collective-permute-start | bytes 18440 | tf_op jit(solution)/shard_map/ppermute | solution.py:15
  3.3 3.0 %copy-start.1 = (f32[4,16]{1,0:T(4,128)S(1)}, f32[4,16]{1,0:T(4,128)}, u32[]{:S(2)}) copy-start(f32[4,16]{1,0:T(4,128)} %param.6) | copy-start | bytes 772
  3.3 7.3 %collective-permute-start.1 = (f32[1,4,3,128]{3,2,1,0:T(4,128)S(1)}, f32[1,4,3,128]{3,2,1,0:T(4,128)S(1)}, u32[]{:S(2)}, u32[]{:S(2)}) collective-permute-start(f32[1,4,3,128]{3,2,1,0:T(4,128)S(1)} %get-tuple-element.44), channel_id=1, source_target_pairs={{1,0},{2,1},{3,2},{4,3},{5,4},{6,5},{7,6},{0,7},{9,8},{10,9},{11,1... | collective-permute-start | bytes 18440 | tf_op jit(solution)/shard_map/ppermute | solution.py:18
  6.3 4.0 %collective-permute-start.2 = (f32[7,4,3]{2,1,0:T(4,128)S(1)}, f32[7,4,3]{2,1,0:T(4,128)S(1)}, u32[]{:S(2)}, u32[]{:S(2)}) collective-permute-start(f32[7,4,3]{2,1,0:T(4,128)S(1)} %get-tuple-element.45), channel_id=1, source_target_pairs={{0,1},{1,2},{2,3},{3,4},{4,5},{5,6},{6,7},{7,0},{8,9},{9,10},{10,1... | collective-permute-start | bytes 1016 | tf_op jit(solution)/shard_map/ppermute | solution.py:15
  6.6 3.8 %collective-permute-start.3 = (f32[7,4,3]{2,1,0:T(4,128)S(1)}, f32[7,4,3]{2,1,0:T(4,128)S(1)}, u32[]{:S(2)}, u32[]{:S(2)}) collective-permute-start(f32[7,4,3]{2,1,0:T(4,128)S(1)} %get-tuple-element.46), channel_id=1, source_target_pairs={{1,0},{2,1},{3,2},{4,3},{5,4},{6,5},{7,6},{0,7},{9,8},{10,9},{11,1... | collective-permute-start | bytes 1016 | tf_op jit(solution)/shard_map/ppermute | solution.py:18
  12.0 9.5 %all-to-all-start = ((f32[8,1,1024]{2,1,0:T(1,128)}), f32[8,1,1024]{2,1,0:T(1,128)S(1)}, u32[]{:S(2)}, u32[]{:S(2)}) async-start(f32[8,1,1024]{2,1,0:T(1,128)} %reshape.186), calls=%async_computation | async-start | bytes 65536 | tf_op jit(solution)/shard_map/all_to_all | solution.py:66
  23.3 9.3 %collective-permute-start.4 = (f32[1,1,128,16]{2,3,1,0:T(8,128)S(1)}, f32[1,1,128,16]{2,3,1,0:T(8,128)S(1)}, u32[]{:S(2)}, u32[]{:S(2)}) collective-permute-start(f32[1,1,128,16]{2,3,1,0:T(8,128)S(1)} %get-tuple-element.42), channel_id=1, source_target_pairs={{0,24},{1,25},{2,26},{3,27},{4,28},{5,29},{6,30},{7,31}} | collective-permute-start | bytes 24584 | tf_op jit(solution)/shard_map/ppermute | solution.py:26
  28.8 3.8 %collective-permute-start.5 = (f32[1,1,128,16]{2,3,1,0:T(8,128)S(1)}, f32[1,1,128,16]{2,3,1,0:T(8,128)S(1)}, u32[]{:S(2)}, u32[]{:S(2)}) collective-permute-start(f32[1,1,128,16]{2,3,1,0:T(8,128)S(1)} %get-tuple-element.41), channel_id=1, source_target_pairs={{0,16},{8,24},{1,17},{9,25},{2,18},{10,26},{3,19},{11,27},{4,20},{... | collective-permute-start | bytes 24584 | tf_op jit(solution)/shard_map/ppermute | solution.py:26
  30.1 3.8 %collective-permute-start.6 = (f32[1,1,128,16]{2,3,1,0:T(8,128)S(1)}, f32[1,1,128,16]{2,3,1,0:T(8,128)S(1)}, u32[]{:S(2)}, u32[]{:S(2)}) collective-permute-start(f32[1,1,128,16]{2,3,1,0:T(8,128)S(1)} %get-tuple-element.40), channel_id=1, source_target_pairs={{0,8},{8,16},{16,24},{1,9},{9,17},{17,25},{2,10},{10,18},{18,26},{... | collective-permute-start | bytes 24584 | tf_op jit(solution)/shard_map/ppermute | solution.py:26
  33.9 5.8 %collective-permute-start.7 = (f32[1,1,128,16]{2,3,1,0:T(8,128)S(1)}, f32[1,1,128,16]{2,3,1,0:T(8,128)S(1)}, u32[]{:S(2)}, u32[]{:S(2)}) collective-permute-start(f32[1,1,128,16]{2,3,1,0:T(8,128)S(1)} %get-tuple-element.38), channel_id=1, source_target_pairs={{8,0},{16,8},{24,16},{9,1},{17,9},{25,17},{10,2},{18,10},{26,18},{... | collective-permute-start | bytes 24584 | tf_op jit(solution)/shard_map/ppermute | solution.py:26
  35.2 7.3 %collective-permute-start.8 = (f32[1,1,128,16]{2,3,1,0:T(8,128)S(1)}, f32[1,1,128,16]{2,3,1,0:T(8,128)S(1)}, u32[]{:S(2)}, u32[]{:S(2)}) collective-permute-start(f32[1,1,128,16]{2,3,1,0:T(8,128)S(1)} %get-tuple-element.37), channel_id=1, source_target_pairs={{16,0},{24,8},{17,1},{25,9},{18,2},{26,10},{19,3},{27,11},{20,4},{... | collective-permute-start | bytes 24584 | tf_op jit(solution)/shard_map/ppermute | solution.py:26
  36.5 8.8 %collective-permute-start.9 = (f32[1,1,128,16]{2,3,1,0:T(8,128)S(1)}, f32[1,1,128,16]{2,3,1,0:T(8,128)S(1)}, u32[]{:S(2)}, u32[]{:S(2)}) collective-permute-start(f32[1,1,128,16]{2,3,1,0:T(8,128)S(1)} %get-tuple-element.36), channel_id=1, source_target_pairs={{24,0},{25,1},{26,2},{27,3},{28,4},{29,5},{30,6},{31,7}} | collective-permute-start | bytes 24584 | tf_op jit(solution)/shard_map/ppermute | solution.py:26
  45.4 4.1 %collective-permute-start.10 = (f32[1,4,3,128]{3,2,1,0:T(4,128)S(1)}, f32[1,4,3,128]{3,2,1,0:T(4,128)S(1)}, u32[]{:S(2)}, u32[]{:S(2)}) collective-permute-start(f32[1,4,3,128]{3,2,1,0:T(4,128)S(1)} %get-tuple-element.34), channel_id=1, source_target_pairs={{0,1},{1,2},{2,3},{3,4},{4,5},{5,6},{6,7},{7,0},{8,9},{9,10},{10,1... | collective-permute-start | bytes 18440 | tf_op jit(solution)/shard_map/ppermute | solution.py:15
  45.4 4.0 %collective-permute-start.11 = (f32[1,4,3,128]{3,2,1,0:T(4,128)S(1)}, f32[1,4,3,128]{3,2,1,0:T(4,128)S(1)}, u32[]{:S(2)}, u32[]{:S(2)}) collective-permute-start(f32[1,4,3,128]{3,2,1,0:T(4,128)S(1)} %get-tuple-element.35), channel_id=1, source_target_pairs={{1,0},{2,1},{3,2},{4,3},{5,4},{6,5},{7,6},{0,7},{9,8},{10,9},{11,1... | collective-permute-start | bytes 18440 | tf_op jit(solution)/shard_map/ppermute | solution.py:18
  60.1 2.6 %collective-permute-start.12 = (f32[1,1,128,16]{2,3,1,0:T(8,128)S(1)}, f32[1,1,128,16]{2,3,1,0:T(8,128)S(1)}, u32[]{:S(2)}, u32[]{:S(2)}) collective-permute-start(f32[1,1,128,16]{2,3,1,0:T(8,128)S(1)} %get-tuple-element.31), channel_id=1, source_target_pairs={{0,8},{8,16},{16,24},{1,9},{9,17},{17,25},{2,10},{10,18},{18,26},{... | collective-permute-start | bytes 24584 | tf_op jit(solution)/shard_map/ppermute | solution.py:26
  61.4 5.5 %collective-permute-start.13 = (f32[1,1,128,16]{2,3,1,0:T(8,128)S(1)}, f32[1,1,128,16]{2,3,1,0:T(8,128)S(1)}, u32[]{:S(2)}, u32[]{:S(2)}) collective-permute-start(f32[1,1,128,16]{2,3,1,0:T(8,128)S(1)} %get-tuple-element.32), channel_id=1, source_target_pairs={{8,0},{16,8},{24,16},{9,1},{17,9},{25,17},{10,2},{18,10},{26,18},{... | collective-permute-start | bytes 24584 | tf_op jit(solution)/shard_map/ppermute | solution.py:26
where the time goes:
time: 68 us; the launch traced here: 67.6 us
  starting transfers between devices  29.2 us (43%)
  waiting for transfers between devices  20.7 us (30%)
  blocking collectives  8.51 us (13%)
  local copies, waits for them, and re-layouts  4.84 us (7%)
  other arithmetic  3.95 us (6%)
    ppermute x8, starting transfers between devices, from_behind(): return lax.ppermute(shard, axis, pairs)  15.7 us
    ppermute x8, waiting for transfers between devices, from_behind(): return lax.ppermute(shard, axis, pairs)  13 us
    all_to_all x1, blocking collectives, relayout(): lax.all_to_all(block, 'lon', split_axis=3, concat_axis=2, tiled=True)  8.51 us
    ppermute x3, starting transfers between devices, extended_2(): lax.ppermute(lax.slice_in_dim(block, 0, width, axis=dim), axis, backward)  7.9 us
    all_to_all x1, waiting for transfers between devices, relayout(): lax.all_to_all(block, 'lon', split_axis=3, concat_axis=2, tiled=True)  4.84 us
    all_to_all x1, starting transfers between devices, relayout(): lax.all_to_all(block, 'lon', split_axis=3, concat_axis=2, tiled=True)  4.63 us
    ppermute x3, waiting for transfers between devices, extended_2(): lax.ppermute(lax.slice_in_dim(block, block.shape[dim] - width, None, axis...  2.77 us
    unnamed x15, local copies, waits for them, and re-layouts  2.15 us
  transfers between devices with their start and end apart: 15, of which 8 were waited for; matrix products, arithmetic and copies ran while one was open for 0% of the time, Pallas kernels for 0%

commit v1 on v0

--- a/solution.py
+++ b/solution.py
@@ -2,6 +2,7 @@
 import jax.numpy as jnp
 from jax import lax
 from jax.sharding import PartitionSpec as P
+from jax.lax import all_to_all, axis_size
 
 STEPS = 3
 
@@ -63,7 +64,9 @@
 def relayout(block, reach_rows):
     row_count = block.shape[0]
     lat_count = block.shape[1]
-    swapped = lax.all_to_all(block, "lon", split_axis=3, concat_axis=2, tiled=True)
+    upper = jnp.split(block, axis_size("lon"), axis=3)
+    later = all_to_all(jnp.stack(upper, axis=0), axis_name="lon", split_axis=0, concat_axis=0)
+    swapped = jnp.concatenate(later, axis=2)
     lon_count = swapped.shape[2]
     col_count = swapped.shape[3]
     block_count = lat_count // row_count

time: 68 us -> 68.5 us (level)
    unnamed x15 -> x29, local copies, waits for them, and re-layouts: 2.15 us -> 2.77 us
where the time goes in v1:
time: 68.5 us; the launch traced here: 68 us
  starting transfers between devices  29.2 us (43%)
  waiting for transfers between devices  20.7 us (30%)
  blocking collectives  8.51 us (12%)
  local copies, waits for them, and re-layouts  5.29 us (8%)
  other arithmetic  3.94 us (6%)
    ppermute x8, starting transfers between devices, from_behind(): return lax.ppermute(shard, axis, pairs)  15.7 us
    ppermute x8, waiting for transfers between devices, from_behind(): return lax.ppermute(shard, axis, pairs)  13 us
    all_to_all x1, blocking collectives, relayout(): all_to_all(jnp.stack(upper, axis=0), axis_name='lon', split_axis=0, conca...  8.51 us
    ppermute x3, starting transfers between devices, extended_2(): lax.ppermute(lax.slice_in_dim(block, 0, width, axis=dim), axis, backward)  7.9 us
    all_to_all x1, waiting for transfers between devices, relayout(): all_to_all(jnp.stack(upper, axis=0), axis_name='lon', split_axis=0, conca...  4.84 us
    all_to_all x1, starting transfers between devices, relayout(): all_to_all(jnp.stack(upper, axis=0), axis_name='lon', split_axis=0, conca...  4.63 us
    ppermute x3, waiting for transfers between devices, extended_2(): lax.ppermute(lax.slice_in_dim(block, block.shape[dim] - width, None, axis...  2.77 us
    unnamed x29, local copies, waits for them, and re-layouts  2.77 us
  transfers between devices with their start and end apart: 15, of which 8 were waited for; matrix products, arithmetic and copies ran while one was open for 0% of the time, Pallas kernels for 0%

profile of v1, /device:TPU:0, one launch (start us, length us, event | category | flops | bytes accessed | tf_op | source)
XLA Modules:
  0.0 68.0 jit_solution(759158874249953331)
XLA Ops:
  0.0 0.7 copy-done.2
  0.7 0.6 dynamic_slice.34
  1.2 0.7 fusion.50
  1.9 0.8 %broadcast_select_fusion = f32[1,4,16,128]{3,2,1,0:T(8,128)S(1)} fusion(f32[1,4,16,128]{3,2,1,0:T(8,128)} %param.4, pred[4]{0:T(512)(128)(4,1)S(1)} %get-tuple-element.51), kind=kLoop, calls=%fused_computation.118 | loop fusion | flops 8192 | bytes 65540 | tf_op jit(solution)/shard_map/jit(_where)/select_n | solution.py:114
  2.7 0.5 collective-permute-start
  3.3 2.9 %collective-permute-start.1 = (f32[1,4,3,128]{3,2,1,0:T(4,128)S(1)}, f32[1,4,3,128]{3,2,1,0:T(4,128)S(1)}, u32[]{:S(2)}, u32[]{:S(2)}) collective-permute-start(f32[1,4,3,128]{3,2,1,0:T(4,128)S(1)} %get-tuple-element.44), channel_id=1, source_target_pairs={{1,0},{2,1},{3,2},{4,3},{5,4},{6,5},{7,6},{0,7},{9,8},{10,9},{11,1... | collective-permute-start | bytes 18440 | tf_op jit(solution)/shard_map/ppermute | solution.py:19
  6.2 0.1 slice_maximum_fusion
  6.3 0.3 collective-permute-start.2
  6.6 2.3 %collective-permute-start.3 = (f32[7,4,3]{2,1,0:T(4,128)S(1)}, f32[7,4,3]{2,1,0:T(4,128)S(1)}, u32[]{:S(2)}, u32[]{:S(2)}) collective-permute-start(f32[7,4,3]{2,1,0:T(4,128)S(1)} %get-tuple-element.46), channel_id=1, source_target_pairs={{1,0},{2,1},{3,2},{4,3},{5,4},{6,5},{7,6},{0,7},{9,8},{10,9},{11,1... | collective-permute-start | bytes 1016 | tf_op jit(solution)/shard_map/ppermute | solution.py:19
  9.0 1.4 %collective-permute-done.2 = f32[7,4,3]{2,1,0:T(4,128)S(1)} collective-permute-done((f32[7,4,3]{2,1,0:T(4,128)S(1)}, f32[7,4,3]{2,1,0:T(4,128)S(1)}, u32[]{:S(2)}, u32[]{:S(2)}) %collective-permute-start.2) | collective-permute-done | bytes 368 | tf_op jit(solution)/shard_map/ppermute | solution.py:16
  10.4 0.1 maximum_bitcast_fusion.6
  10.5 0.1 maximum_bitcast_fusion.4
  10.6 0.1 fusion.4
  10.8 0.1 fusion.12
  10.9 0.1 fusion.36
  11.1 0.1 constant_dynamic-update-slice_fusion.6
  11.1 0.1 constant_dynamic-update-slice_fusion.5
  11.2 0.1 constant_dynamic-update-slice_fusion.4
  11.3 0.1 constant_dynamic-update-slice_fusion.3
  11.4 0.1 constant_dynamic-update-slice_fusion.2
  11.4 0.1 constant_dynamic-update-slice_fusion.1
  11.5 0.1 constant_dynamic-update-slice_fusion
  11.6 0.8 %reshape.184 = f32[8,1,1024]{2,1,0:T(1,128)} reshape(f32[8,1,4,16,16]{4,3,2,1,0:T(8,128)S(1)} %constant_dynamic-update-slice_fusion) | data formatting | bytes 65536
  12.4 4.6 %all-to-all-start = ((f32[8,1,1024]{2,1,0:T(1,128)}), f32[8,1,1024]{2,1,0:T(1,128)S(1)}, u32[]{:S(2)}, u32[]{:S(2)}) async-start(f32[8,1,1024]{2,1,0:T(1,128)} %reshape.184), calls=%async_computation | async-start | bytes 65536 | tf_op jit(solution)/shard_map/all_to_all | solution.py:68
  17.0 4.8 %all-to-all-done = f32[8,1,1024]{2,1,0:T(1,128)S(1)} async-done(((f32[8,1,1024]{2,1,0:T(1,128)}), f32[8,1,1024]{2,1,0:T(1,128)S(1)}, u32[]{:S(2)}, u32[]{:S(2)}) %all-to-all-start) | async-done | bytes 32800 | tf_op jit(solution)/shard_map/all_to_all | solution.py:68
  21.8 0.5 broadcast.178
  22.4 0.7 %reduce = f32[8,1024]{1,0:T(8,128)S(1)} reduce(f32[8,1,1024]{2,1,0:T(1,128)S(1)} %all-to-all-done, f32[]{:T(128)} %broadcast.178), dimensions={1}, to_apply=%all_to_all.6.reduce_sub_computation | reduce | bytes 65540 | tf_op jit(solution)/shard_map/all_to_all | solution.py:68
  23.1 0.1 reshape.185
  23.2 0.1 copy.6
  23.4 0.1 reshape_reshape.6
  23.5 5.5 %collective-permute-start.4 = (f32[1,1,128,16]{2,3,1,0:T(8,128)S(1)}, f32[1,1,128,16]{2,3,1,0:T(8,128)S(1)}, u32[]{:S(2)}, u32[]{:S(2)}) collective-permute-start(f32[1,1,128,16]{2,3,1,0:T(8,128)S(1)} %get-tuple-element.42), channel_id=1, source_target_pairs={{0,24},{1,25},{2,26},{3,27},{4,28},{5,29},{6,30},{7,31}} | collective-permute-start | bytes 24584 | tf_op jit(solution)/shard_map/ppermute | solution.py:27
  29.0 1.3 %collective-permute-start.5 = (f32[1,1,128,16]{2,3,1,0:T(8,128)S(1)}, f32[1,1,128,16]{2,3,1,0:T(8,128)S(1)}, u32[]{:S(2)}, u32[]{:S(2)}) collective-permute-start(f32[1,1,128,16]{2,3,1,0:T(8,128)S(1)} %get-tuple-element.41), channel_id=1, source_target_pairs={{0,16},{8,24},{1,17},{9,25},{2,18},{10,26},{3,19},{11,27},{4,20},{... | collective-permute-start | bytes 24584 | tf_op jit(solution)/shard_map/ppermute | solution.py:27
  30.3 2.5 %collective-permute-start.6 = (f32[1,1,128,16]{2,3,1,0:T(8,128)S(1)}, f32[1,1,128,16]{2,3,1,0:T(8,128)S(1)}, u32[]{:S(2)}, u32[]{:S(2)}) collective-permute-start(f32[1,1,128,16]{2,3,1,0:T(8,128)S(1)} %get-tuple-element.40), channel_id=1, source_target_pairs={{0,8},{8,16},{16,24},{1,9},{9,17},{17,25},{2,10},{10,18},{18,26},{... | collective-permute-start | bytes 24584 | tf_op jit(solution)/shard_map/ppermute | solution.py:27
  32.9 1.3 %collective-permute-done.6 = f32[1,1,128,16]{2,3,1,0:T(8,128)S(1)} collective-permute-done((f32[1,1,128,16]{2,3,1,0:T(8,128)S(1)}, f32[1,1,128,16]{2,3,1,0:T(8,128)S(1)}, u32[]{:S(2)}, u32[]{:S(2)}) %collective-permute-start.6) | collective-permute-done | bytes 8224 | tf_op jit(solution)/shard_map/ppermute | solution.py:27
  34.2 1.3 %collective-permute-start.7 = (f32[1,1,128,16]{2,3,1,0:T(8,128)S(1)}, f32[1,1,128,16]{2,3,1,0:T(8,128)S(1)}, u32[]{:S(2)}, u32[]{:S(2)}) collective-permute-start(f32[1,1,128,16]{2,3,1,0:T(8,128)S(1)} %get-tuple-element.38), channel_id=1, source_target_pairs={{8,0},{16,8},{24,16},{9,1},{17,9},{25,17},{10,2},{18,10},{26,18},{... | collective-permute-start | bytes 24584 | tf_op jit(solution)/shard_map/ppermute | solution.py:27
  35.5 1.3 %collective-permute-start.8 = (f32[1,1,128,16]{2,3,1,0:T(8,128)S(1)}, f32[1,1,128,16]{2,3,1,0:T(8,128)S(1)}, u32[]{:S(2)}, u32[]{:S(2)}) collective-permute-start(f32[1,1,128,16]{2,3,1,0:T(8,128)S(1)} %get-tuple-element.37), channel_id=1, source_target_pairs={{16,0},{24,8},{17,1},{25,9},{18,2},{26,10},{19,3},{27,11},{20,4},{... | collective-permute-start | bytes 24584 | tf_op jit(solution)/shard_map/ppermute | solution.py:27
  36.8 1.3 %collective-permute-start.9 = (f32[1,1,128,16]{2,3,1,0:T(8,128)S(1)}, f32[1,1,128,16]{2,3,1,0:T(8,128)S(1)}, u32[]{:S(2)}, u32[]{:S(2)}) collective-permute-start(f32[1,1,128,16]{2,3,1,0:T(8,128)S(1)} %get-tuple-element.36), channel_id=1, source_target_pairs={{24,0},{25,1},{26,2},{27,3},{28,4},{29,5},{30,6},{31,7}} | collective-permute-start | bytes 24584 | tf_op jit(solution)/shard_map/ppermute | solution.py:27
  38.1 1.9 %collective-permute-done.7 = f32[1,1,128,16]{2,3,1,0:T(8,128)S(1)} collective-permute-done((f32[1,1,128,16]{2,3,1,0:T(8,128)S(1)}, f32[1,1,128,16]{2,3,1,0:T(8,128)S(1)}, u32[]{:S(2)}, u32[]{:S(2)}) %collective-permute-start.7) | collective-permute-done | bytes 8224 | tf_op jit(solution)/shard_map/ppermute | solution.py:27
  40.0 2.7 %collective-permute-done.8 = f32[1,1,128,16]{2,3,1,0:T(8,128)S(1)} collective-permute-done((f32[1,1,128,16]{2,3,1,0:T(8,128)S(1)}, f32[1,1,128,16]{2,3,1,0:T(8,128)S(1)}, u32[]{:S(2)}, u32[]{:S(2)}) %collective-permute-start.8) | collective-permute-done | bytes 8224 | tf_op jit(solution)/shard_map/ppermute | solution.py:27
  42.7 2.8 %collective-permute-done.9 = f32[1,1,128,16]{2,3,1,0:T(8,128)S(1)} collective-permute-done((f32[1,1,128,16]{2,3,1,0:T(8,128)S(1)}, f32[1,1,128,16]{2,3,1,0:T(8,128)S(1)}, u32[]{:S(2)}, u32[]{:S(2)}) %collective-permute-start.9) | collective-permute-done | bytes 8224 | tf_op jit(solution)/shard_map/ppermute | solution.py:27
  45.6 0.1 collective-permute-start.10
  45.7 2.6 %collective-permute-start.11 = (f32[1,4,3,128]{3,2,1,0:T(4,128)S(1)}, f32[1,4,3,128]{3,2,1,0:T(4,128)S(1)}, u32[]{:S(2)}, u32[]{:S(2)}) collective-permute-start(f32[1,4,3,128]{3,2,1,0:T(4,128)S(1)} %get-tuple-element.35), channel_id=1, source_target_pairs={{1,0},{2,1},{3,2},{4,3},{5,4},{6,5},{7,6},{0,7},{9,8},{10,9},{11,1... | collective-permute-start | bytes 18440 | tf_op jit(solution)/shard_map/ppermute | solution.py:19
  48.3 1.4 %collective-permute-done.10 = f32[1,4,3,128]{3,2,1,0:T(4,128)S(1)} collective-permute-done((f32[1,4,3,128]{3,2,1,0:T(4,128)S(1)}, f32[1,4,3,128]{3,2,1,0:T(4,128)S(1)}, u32[]{:S(2)}, u32[]{:S(2)}) %collective-permute-start.10) | collective-permute-done | bytes 6176 | tf_op jit(solution)/shard_map/ppermute | solution.py:16
  49.7 0.1 fusion.20
  49.9 0.1 fusion.28
  50.0 0.1 fusion.45
  50.2 0.1 constant_dynamic-update-slice_fusion.21
  50.2 0.1 constant_dynamic-update-slice_fusion.20
  50.3 0.1 constant_dynamic-update-slice_fusion.19
  50.4 0.1 constant_dynamic-update-slice_fusion.18
  50.5 0.1 constant_dynamic-update-slice_fusion.17
  50.5 0.1 constant_dynamic-update-slice_fusion.16
  50.6 0.1 constant_dynamic-update-slice_fusion.15
  50.7 0.2 reshape.186
  50.9 8.5 %all_to_all.10 = f32[8,1,1024]{2,1,0:T(1,128)S(1)} all-to-all(f32[8,1,1024]{2,1,0:T(1,128)S(1)} %reshape.186), channel_id=1, replica_groups=mesh['lat'=4,'lon'=8] {'lon'}, dimensions={0} | all-to-all | bytes 65536 | tf_op jit(solution)/shard_map/all_to_all | solution.py:68
  59.4 0.7 %reduce.1 = f32[8,1024]{1,0:T(8,128)S(1)} reduce(f32[8,1,1024]{2,1,0:T(1,128)S(1)} %all_to_all.10, f32[]{:T(128)} %broadcast.178), dimensions={1}, to_apply=%all_to_all.7.reduce_sub_computation | reduce | bytes 65540 | tf_op jit(solution)/shard_map/all_to_all | solution.py:68
  60.1 0.1 reshape.187
  60.2 0.1 copy.8
  60.4 0.1 reshape_reshape.7
  60.5 1.3 %collective-permute-start.12 = (f32[1,1,128,16]{2,3,1,0:T(8,128)S(1)}, f32[1,1,128,16]{2,3,1,0:T(8,128)S(1)}, u32[]{:S(2)}, u32[]{:S(2)}) collective-permute-start(f32[1,1,128,16]{2,3,1,0:T(8,128)S(1)} %get-tuple-element.31), channel_id=1, source_target_pairs={{0,8},{8,16},{16,24},{1,9},{9,17},{17,25},{2,10},{10,18},{18,26},{... | collective-permute-start | bytes 24584 | tf_op jit(solution)/shard_map/ppermute | solution.py:27
  61.8 1.3 %collective-permute-start.13 = (f32[1,1,128,16]{2,3,1,0:T(8,128)S(1)}, f32[1,1,128,16]{2,3,1,0:T(8,128)S(1)}, u32[]{:S(2)}, u32[]{:S(2)}) collective-permute-start(f32[1,1,128,16]{2,3,1,0:T(8,128)S(1)} %get-tuple-element.32), channel_id=1, source_target_pairs={{8,0},{16,8},{24,16},{9,1},{17,9},{25,17},{10,2},{18,10},{26,18},{... | collective-permute-start | bytes 24584 | tf_op jit(solution)/shard_map/ppermute | solution.py:27
  63.1 0.0 collective-permute-done.12
  63.2 4.2 %collective-permute-done.13 = f32[1,1,128,16]{2,3,1,0:T(8,128)S(1)} collective-permute-done((f32[1,1,128,16]{2,3,1,0:T(8,128)S(1)}, f32[1,1,128,16]{2,3,1,0:T(8,128)S(1)}, u32[]{:S(2)}, u32[]{:S(2)}) %collective-permute-start.13) | collective-permute-done | bytes 8224 | tf_op jit(solution)/shard_map/ppermute | solution.py:27
  67.4 0.6 slice_bitcast_fusion
  (40 shorter events, 0.2 us)
Async XLA Ops:
  0.0 0.7 copy-start.2
  2.7 3.5 %copy-start = (f32[2,3,4,16]{3,2,1,0:T(4,128)S(1)}, f32[2,3,4,16]{3,2,1,0:T(4,128)}, u32[]{:S(2)}) copy-start(f32[2,3,4,16]{3,2,1,0:T(4,128)} %param.5) | copy-start | bytes 4612
  2.7 7.8 %collective-permute-start = (f32[1,4,3,128]{3,2,1,0:T(4,128)S(1)}, f32[1,4,3,128]{3,2,1,0:T(4,128)S(1)}, u32[]{:S(2)}, u32[]{:S(2)}) collective-permute-start(f32[1,4,3,128]{3,2,1,0:T(4,128)S(1)} %get-tuple-element.43), channel_id=1, source_target_pairs={{0,1},{1,2},{2,3},{3,4},{4,5},{5,6},{6,7},{7,0},{8,9},{9,10},{10,1... | collective-permute-start | bytes 18440 | tf_op jit(solution)/shard_map/ppermute | solution.py:16
  3.3 3.0 %copy-start.1 = (f32[4,16]{1,0:T(4,128)S(1)}, f32[4,16]{1,0:T(4,128)}, u32[]{:S(2)}) copy-start(f32[4,16]{1,0:T(4,128)} %param.6) | copy-start | bytes 772
  3.3 7.3 %collective-permute-start.1 = (f32[1,4,3,128]{3,2,1,0:T(4,128)S(1)}, f32[1,4,3,128]{3,2,1,0:T(4,128)S(1)}, u32[]{:S(2)}, u32[]{:S(2)}) collective-permute-start(f32[1,4,3,128]{3,2,1,0:T(4,128)S(1)} %get-tuple-element.44), channel_id=1, source_target_pairs={{1,0},{2,1},{3,2},{4,3},{5,4},{6,5},{7,6},{0,7},{9,8},{10,9},{11,1... | collective-permute-start | bytes 18440 | tf_op jit(solution)/shard_map/ppermute | solution.py:19
  6.3 4.0 %collective-permute-start.2 = (f32[7,4,3]{2,1,0:T(4,128)S(1)}, f32[7,4,3]{2,1,0:T(4,128)S(1)}, u32[]{:S(2)}, u32[]{:S(2)}) collective-permute-start(f32[7,4,3]{2,1,0:T(4,128)S(1)} %get-tuple-element.45), channel_id=1, source_target_pairs={{0,1},{1,2},{2,3},{3,4},{4,5},{5,6},{6,7},{7,0},{8,9},{9,10},{10,1... | collective-permute-start | bytes 1016 | tf_op jit(solution)/shard_map/ppermute | solution.py:16
  6.6 3.8 %collective-permute-start.3 = (f32[7,4,3]{2,1,0:T(4,128)S(1)}, f32[7,4,3]{2,1,0:T(4,128)S(1)}, u32[]{:S(2)}, u32[]{:S(2)}) collective-permute-start(f32[7,4,3]{2,1,0:T(4,128)S(1)} %get-tuple-element.46), channel_id=1, source_target_pairs={{1,0},{2,1},{3,2},{4,3},{5,4},{6,5},{7,6},{0,7},{9,8},{10,9},{11,1... | collective-permute-start | bytes 1016 | tf_op jit(solution)/shard_map/ppermute | solution.py:19
  12.4 9.5 %all-to-all-start = ((f32[8,1,1024]{2,1,0:T(1,128)}), f32[8,1,1024]{2,1,0:T(1,128)S(1)}, u32[]{:S(2)}, u32[]{:S(2)}) async-start(f32[8,1,1024]{2,1,0:T(1,128)} %reshape.184), calls=%async_computation | async-start | bytes 65536 | tf_op jit(solution)/shard_map/all_to_all | solution.py:68
  23.5 9.3 %collective-permute-start.4 = (f32[1,1,128,16]{2,3,1,0:T(8,128)S(1)}, f32[1,1,128,16]{2,3,1,0:T(8,128)S(1)}, u32[]{:S(2)}, u32[]{:S(2)}) collective-permute-start(f32[1,1,128,16]{2,3,1,0:T(8,128)S(1)} %get-tuple-element.42), channel_id=1, source_target_pairs={{0,24},{1,25},{2,26},{3,27},{4,28},{5,29},{6,30},{7,31}} | collective-permute-start | bytes 24584 | tf_op jit(solution)/shard_map/ppermute | solution.py:27
  29.0 3.8 %collective-permute-start.5 = (f32[1,1,128,16]{2,3,1,0:T(8,128)S(1)}, f32[1,1,128,16]{2,3,1,0:T(8,128)S(1)}, u32[]{:S(2)}, u32[]{:S(2)}) collective-permute-start(f32[1,1,128,16]{2,3,1,0:T(8,128)S(1)} %get-tuple-element.41), channel_id=1, source_target_pairs={{0,16},{8,24},{1,17},{9,25},{2,18},{10,26},{3,19},{11,27},{4,20},{... | collective-permute-start | bytes 24584 | tf_op jit(solution)/shard_map/ppermute | solution.py:27
  30.3 3.8 %collective-permute-start.6 = (f32[1,1,128,16]{2,3,1,0:T(8,128)S(1)}, f32[1,1,128,16]{2,3,1,0:T(8,128)S(1)}, u32[]{:S(2)}, u32[]{:S(2)}) collective-permute-start(f32[1,1,128,16]{2,3,1,0:T(8,128)S(1)} %get-tuple-element.40), channel_id=1, source_target_pairs={{0,8},{8,16},{16,24},{1,9},{9,17},{17,25},{2,10},{10,18},{18,26},{... | collective-permute-start | bytes 24584 | tf_op jit(solution)/shard_map/ppermute | solution.py:27
  34.2 5.8 %collective-permute-start.7 = (f32[1,1,128,16]{2,3,1,0:T(8,128)S(1)}, f32[1,1,128,16]{2,3,1,0:T(8,128)S(1)}, u32[]{:S(2)}, u32[]{:S(2)}) collective-permute-start(f32[1,1,128,16]{2,3,1,0:T(8,128)S(1)} %get-tuple-element.38), channel_id=1, source_target_pairs={{8,0},{16,8},{24,16},{9,1},{17,9},{25,17},{10,2},{18,10},{26,18},{... | collective-permute-start | bytes 24584 | tf_op jit(solution)/shard_map/ppermute | solution.py:27
  35.5 7.3 %collective-permute-start.8 = (f32[1,1,128,16]{2,3,1,0:T(8,128)S(1)}, f32[1,1,128,16]{2,3,1,0:T(8,128)S(1)}, u32[]{:S(2)}, u32[]{:S(2)}) collective-permute-start(f32[1,1,128,16]{2,3,1,0:T(8,128)S(1)} %get-tuple-element.37), channel_id=1, source_target_pairs={{16,0},{24,8},{17,1},{25,9},{18,2},{26,10},{19,3},{27,11},{20,4},{... | collective-permute-start | bytes 24584 | tf_op jit(solution)/shard_map/ppermute | solution.py:27
  36.8 8.8 %collective-permute-start.9 = (f32[1,1,128,16]{2,3,1,0:T(8,128)S(1)}, f32[1,1,128,16]{2,3,1,0:T(8,128)S(1)}, u32[]{:S(2)}, u32[]{:S(2)}) collective-permute-start(f32[1,1,128,16]{2,3,1,0:T(8,128)S(1)} %get-tuple-element.36), channel_id=1, source_target_pairs={{24,0},{25,1},{26,2},{27,3},{28,4},{29,5},{30,6},{31,7}} | collective-permute-start | bytes 24584 | tf_op jit(solution)/shard_map/ppermute | solution.py:27
  45.6 4.1 %collective-permute-start.10 = (f32[1,4,3,128]{3,2,1,0:T(4,128)S(1)}, f32[1,4,3,128]{3,2,1,0:T(4,128)S(1)}, u32[]{:S(2)}, u32[]{:S(2)}) collective-permute-start(f32[1,4,3,128]{3,2,1,0:T(4,128)S(1)} %get-tuple-element.34), channel_id=1, source_target_pairs={{0,1},{1,2},{2,3},{3,4},{4,5},{5,6},{6,7},{7,0},{8,9},{9,10},{10,1... | collective-permute-start | bytes 18440 | tf_op jit(solution)/shard_map/ppermute | solution.py:16
  45.7 4.0 %collective-permute-start.11 = (f32[1,4,3,128]{3,2,1,0:T(4,128)S(1)}, f32[1,4,3,128]{3,2,1,0:T(4,128)S(1)}, u32[]{:S(2)}, u32[]{:S(2)}) collective-permute-start(f32[1,4,3,128]{3,2,1,0:T(4,128)S(1)} %get-tuple-element.35), channel_id=1, source_target_pairs={{1,0},{2,1},{3,2},{4,3},{5,4},{6,5},{7,6},{0,7},{9,8},{10,9},{11,1... | collective-permute-start | bytes 18440 | tf_op jit(solution)/shard_map/ppermute | solution.py:19
  60.5 2.6 %collective-permute-start.12 = (f32[1,1,128,16]{2,3,1,0:T(8,128)S(1)}, f32[1,1,128,16]{2,3,1,0:T(8,128)S(1)}, u32[]{:S(2)}, u32[]{:S(2)}) collective-permute-start(f32[1,1,128,16]{2,3,1,0:T(8,128)S(1)} %get-tuple-element.31), channel_id=1, source_target_pairs={{0,8},{8,16},{16,24},{1,9},{9,17},{17,25},{2,10},{10,18},{18,26},{... | collective-permute-start | bytes 24584 | tf_op jit(solution)/shard_map/ppermute | solution.py:27
  61.8 5.5 %collective-permute-start.13 = (f32[1,1,128,16]{2,3,1,0:T(8,128)S(1)}, f32[1,1,128,16]{2,3,1,0:T(8,128)S(1)}, u32[]{:S(2)}, u32[]{:S(2)}) collective-permute-start(f32[1,1,128,16]{2,3,1,0:T(8,128)S(1)} %get-tuple-element.32), channel_id=1, source_target_pairs={{8,0},{16,8},{24,16},{9,1},{17,9},{25,17},{10,2},{18,10},{26,18},{... | collective-permute-start | bytes 24584 | tf_op jit(solution)/shard_map/ppermute | solution.py:27
